TPU v7x, 32 devices: a whole 2x2x4 slice. The times are simulated.
32 devices in a mesh: expert: 8 (over z, x), dp: 4 (over y, core).
Axes of the slice: x: 2, y: 2, z: 4, core: 2. Of those that a mesh axis runs over, the one named last changes fastest.
Arguments:
- enc_state: bfloat16 [4, 8, 256, 1024], P('dp', 'expert'), may hold values from -6 to 6
- baseline: bfloat16 [4, 8, 256, 1024], P('dp', 'expert'), may hold values from -6 to 6
- enc_keys: bfloat16 [4, 8, 256, 1024], P('dp', 'expert'), may hold values from -4 to 4
- dec_queries: bfloat16 [4, 8, 128, 1024], P('dp', 'expert'), may hold values from -200 to 200
- out_mult: bfloat16 [4, 8, 128, 1024], P('dp', 'expert'), may hold values from -6 to 6
- doc_lengths: int32 [4, 8], P('dp', 'expert'), may hold values from 128 to 256, as said below
- expert_ids: int32 [4, 8, 256], P('dp', 'expert'), may hold values from 0 to 15
- slot_ids: int32 [4, 8, 256], P('dp', 'expert'), may hold values from 0 to 31, as said below
- gate_prob: float32 [4, 8, 256], P('dp', 'expert'), may hold values from 0.2 to 1
- norm_gain: float32 [1024], replicated, may hold values from 0.5 to 2
- w_in: bfloat16 [16, 1024, 2816], P('expert', None, 'dp'), may hold values from -0.1875 to 0.1875
- w_out_t: bfloat16 [16, 1024, 2816], P('expert', None, 'dp'), may hold values from -0.109375 to 0.109375
- w_value: bfloat16 [1024, 1024], replicated, may hold values from -0.1875 to 0.1875
Outputs:
- enc_mult: bfloat16 [4, 8, 256, 1024], P('dp', 'expert')
Inputs may be any that keep to these rules, and one draw needn't show every extreme that they name: `slot_ids`: within one document no two tokens share an expert and a slot, and every token has a slot; one expert has all 32 slots used in every document. `doc_lengths`: some document has all 256 tokens.
All inputs are finite; a program needn't handle non-finite values.
Results may differ from a plain program's by a relative error of at most 0.0069.
Values may be sent and summed in bfloat16 or wider, within the bound.
A program may use at most 128 MiB of HBM per device.

v0:
```python
import math
import jax
import jax.numpy as jnp
from jax import lax
from jax.sharding import PartitionSpec as P

HEADS = 16
HEAD_DIM = 64


def rescale(pre_act, base_act):
    upper_part = jnp.maximum(jnp.maximum(pre_act, base_act), 0.0)
    lower_part = jnp.maximum(-jnp.minimum(pre_act, base_act), 0.0)
    return upper_part / (upper_part + lower_part + jnp.where(upper_part > 0.0, 0.0, 1.0))


def attend(query_rows, key_rows, mult_rows, length, w_value):
    enc_len = key_rows.shape[0]
    dec_len = query_rows.shape[0]
    queries = query_rows.reshape(dec_len, HEADS, HEAD_DIM)
    keys = key_rows.reshape(enc_len, HEADS, HEAD_DIM)
    mults = mult_rows.reshape(dec_len, HEADS, HEAD_DIM)
    scores = jnp.einsum("qhd,khd->hqk", queries, keys, preferred_element_type=jnp.float32) * (
        1.0 / math.sqrt(HEAD_DIM)
    )
    valid = jnp.arange(enc_len, dtype=jnp.int32) < length
    scores = jnp.where(valid[None, None, :], scores, -jnp.inf)
    top_score = jnp.max(scores, axis=-1, keepdims=True)
    expo = jnp.exp(scores - top_score)
    attn = (expo / jnp.sum(expo, axis=-1, keepdims=True)).astype(jnp.bfloat16)
    value_mult = jnp.einsum("hqk,qhd->khd", attn, mults, preferred_element_type=jnp.float32).astype(
        jnp.bfloat16
    )
    return lax.dot_general(
        value_mult.reshape(enc_len, HEADS * HEAD_DIM),
        w_value,
        (((1,), (1,)), ((), ())),
        preferred_element_type=jnp.float32,
    )


def expert_terms(rows_in, rows_base, rows_mult, part_in, part_out):
    pre_act = jnp.einsum("erd,edf->erf", rows_in, part_in, preferred_element_type=jnp.float32)
    base_act = jnp.einsum("erd,edf->erf", rows_base, part_in, preferred_element_type=jnp.float32)
    hidden_mult = jnp.einsum(
        "erd,edf->erf", rows_mult, part_out, preferred_element_type=jnp.float32
    )
    act_mult = (rescale(pre_act, base_act) * hidden_mult).astype(jnp.bfloat16)
    return jnp.einsum("erf,edf->erd", act_mult, part_in, preferred_element_type=jnp.float32)


def body(
    enc_state,
    baseline,
    enc_keys,
    dec_queries,
    out_mult,
    doc_lengths,
    expert_ids,
    slot_ids,
    gate_prob,
    norm_gain,
    w_in,
    w_out_t,
    w_value,
):
    enc_len = enc_state.shape[2]
    feature_width = enc_state.shape[3]
    local_experts = w_in.shape[0]
    n_experts = local_experts * lax.axis_size("expert")
    n_dp = lax.axis_size("dp")
    near = 2 if n_dp % 2 == 0 else 1
    capacity = max(2, 2 * enc_len // n_experts)
    shards = [(w_in, w_out_t)]
    if near == 2:
        swap = [(i, i ^ 1) for i in range(n_dp)]
        shards.append((lax.ppermute(w_in, "dp", swap), lax.ppermute(w_out_t, "dp", swap)))
    tokens = enc_state[0, 0].astype(jnp.float32)
    row_scale = norm_gain * lax.rsqrt(jnp.mean(tokens * tokens, axis=-1, keepdims=True) + 1e-06)
    inputs = (tokens * row_scale).astype(jnp.bfloat16)
    base_inputs = (baseline[0, 0].astype(jnp.float32) * row_scale).astype(jnp.bfloat16)
    flat_slot = expert_ids[0, 0] * capacity + slot_ids[0, 0]
    onehot = (
        flat_slot[None, :] == jnp.arange(n_experts * capacity, dtype=jnp.int32)[:, None]
    ).astype(jnp.bfloat16)

    def dispatch(values):
        placed = jnp.dot(onehot, values, preferred_element_type=jnp.float32).astype(jnp.bfloat16)
        placed = placed.reshape(n_experts, capacity, feature_width)
        return lax.all_to_all(placed, "expert", split_axis=0, concat_axis=1, tiled=True)

    sent_in = dispatch(inputs)
    sent_base = dispatch(base_inputs)
    layer_mult = attend(
        dec_queries[0, 0], enc_keys[0, 0], out_mult[0, 0], doc_lengths[0, 0], w_value
    )
    scaled_mult = (gate_prob[0, 0][:, None] * layer_mult).astype(jnp.bfloat16)
    sent_mult = dispatch(scaled_mult)
    own_rows = (sent_in, sent_base, sent_mult)

    def partial_sum(rows):
        total = expert_terms(*rows, *shards[0])
        for part in shards[1:]:
            total = total + expert_terms(*rows, *part)
        return total

    far = n_dp // near
    far_rows = []
    for hop in range(1, far):
        ahead = [(i, (i + hop * near) % n_dp) for i in range(n_dp)]
        far_rows.append(tuple((lax.ppermute(a, "dp", ahead) for a in own_rows)))
    slot_mult = partial_sum(own_rows)
    for hop in range(1, far):
        back = [((i + hop * near) % n_dp, i) for i in range(n_dp)]
        far_part = partial_sum(far_rows[hop - 1]).astype(jnp.bfloat16)
        slot_mult = slot_mult + lax.ppermute(far_part, "dp", back).astype(jnp.float32)
    returned = lax.all_to_all(
        slot_mult.astype(jnp.bfloat16), "expert", split_axis=1, concat_axis=0, tiled=True
    )
    per_token = lax.dot_general(
        onehot,
        returned.reshape(n_experts * capacity, feature_width),
        (((0,), (0,)), ((), ())),
        preferred_element_type=jnp.float32,
    )
    result = (layer_mult + row_scale * per_token).astype(jnp.bfloat16)
    return result[None, None]


def solution(mesh):
    in_specs = (
        P("dp", "expert", None, None),
        P("dp", "expert", None, None),
        P("dp", "expert", None, None),
        P("dp", "expert", None, None),
        P("dp", "expert", None, None),
        P("dp", "expert"),
        P("dp", "expert", None),
        P("dp", "expert", None),
        P("dp", "expert", None),
        P(),
        P("expert", None, "dp"),
        P("expert", None, "dp"),
        P(),
    )
    out_specs = P("dp", "expert", None, None)
    return jax.shard_map(body, mesh=mesh, in_specs=in_specs, out_specs=out_specs, check_vma=False)
```

profile of v0, /device:TPU:0, one launch (start us, length us, event | category | flops | bytes accessed | tf_op | source)
XLA Modules:
  0.0 234.2 jit_solution(12042869311677658196)
XLA Ops:
  0.0 1.4 copy.40
  1.4 1.1 copy.39
  3.2 1.1 copy.41
  4.3 2.0 fusion.48
  6.3 2.1 convolution_convert_fusion.3
  8.5 0.0 copy-start.5
  8.5 0.8 fusion.55
  9.4 0.0 copy-start.3
  9.4 1.5 convolution_convert_fusion
  10.9 7.3 %all-to-all-start.2 = ((bf16[16,32,1024]{2,1,0:T(8,128)(2,1)}), bf16[16,32,1024]{2,1,0:T(8,128)(2,1)}, u32[]{:S(2)}, u32[]{:S(2)}) async-start(bf16[16,32,1024]{2,1,0:T(8,128)(2,1)} %bitcast.78), calls=%async_computation.2 | async-start | bytes 2097152 | tf_op jit(solution)/shard_map/all_to_all | solution.py:90
  18.1 1.2 fusion.7
  19.4 2.6 %convolution_convert_fusion.2 = bf16[512,1024]{1,0:T(8,128)(2,1)} fusion(bf16[1,1,256,1024]{3,2,1,0:T(8,128)(2,1)} %param.13, f32[256]{0:T(256)S(1)} %add_rsqrt_fusion, f32[1024]{0:T(1024)S(1)} %copy-done.3, s32[256]{0:T(256)S(1)} %bitcast.88), kind=kOutput, calls=%fused_computation.12 | convolution fusion | flops 270139392 | bytes 1579008 | tf_op jit(solution)/shard_map/dot_general | solution.py:88
  22.0 22.0 %all-to-all-done.2 = bf16[16,32,1024]{2,1,0:T(8,128)(2,1)} async-done(((bf16[16,32,1024]{2,1,0:T(8,128)(2,1)}), bf16[16,32,1024]{2,1,0:T(8,128)(2,1)}, u32[]{:S(2)}, u32[]{:S(2)}) %all-to-all-start.2) | async-done | bytes 1048608 | tf_op jit(solution)/shard_map/all_to_all | solution.py:90
  44.0 4.2 %all-to-all-start = ((bf16[16,32,1024]{2,1,0:T(8,128)(2,1)}), bf16[16,32,1024]{2,1,0:T(8,128)(2,1)}, u32[]{:S(2)}, u32[]{:S(2)}) async-start(bf16[16,32,1024]{2,1,0:T(8,128)(2,1)} %bitcast.82), calls=%async_computation | async-start | bytes 2097152 | tf_op jit(solution)/shard_map/all_to_all | solution.py:90
  48.3 2.6 %convolution_convert_fusion.1 = bf16[512,1024]{1,0:T(8,128)(2,1)} fusion(bf16[1,1,256,1024]{3,2,1,0:T(8,128)(2,1)} %param.14, f32[256]{0:T(256)S(1)} %add_rsqrt_fusion, f32[1024]{0:T(1024)S(1)} %copy-done.3, s32[256]{0:T(256)S(1)} %bitcast.89), kind=kOutput, calls=%fused_computation.11 | convolution fusion | flops 270139392 | bytes 1579008 | tf_op jit(solution)/shard_map/dot_general | solution.py:88
  50.8 23.0 %all-to-all-done = bf16[16,32,1024]{2,1,0:T(8,128)(2,1)} async-done(((bf16[16,32,1024]{2,1,0:T(8,128)(2,1)}), bf16[16,32,1024]{2,1,0:T(8,128)(2,1)}, u32[]{:S(2)}, u32[]{:S(2)}) %all-to-all-start) | async-done | bytes 1048608 | tf_op jit(solution)/shard_map/all_to_all | solution.py:90
  73.8 4.4 %all-to-all-start.1 = ((bf16[16,32,1024]{2,1,0:T(8,128)(2,1)}), bf16[16,32,1024]{2,1,0:T(8,128)(2,1)}, u32[]{:S(2)}, u32[]{:S(2)}) async-start(bf16[16,32,1024]{2,1,0:T(8,128)(2,1)} %bitcast.81), calls=%async_computation.1 | async-start | bytes 2097152 | tf_op jit(solution)/shard_map/all_to_all | solution.py:90
  78.3 0.1 collective-permute-start
  78.4 0.5 collective-permute-start.1
  78.8 2.3 copy.44
  81.1 1.5 collective-permute-start.4
  82.7 2.3 copy.42
  85.0 0.5 collective-permute-start.2
  85.5 18.1 %all-to-all-done.1 = bf16[16,32,1024]{2,1,0:T(8,128)(2,1)} async-done(((bf16[16,32,1024]{2,1,0:T(8,128)(2,1)}), bf16[16,32,1024]{2,1,0:T(8,128)(2,1)}, u32[]{:S(2)}, u32[]{:S(2)}) %all-to-all-start.1) | async-done | bytes 1048608 | tf_op jit(solution)/shard_map/all_to_all | solution.py:90
  103.5 2.3 copy.43
  105.8 1.5 collective-permute-start.3
  107.3 4.3 %fusion.56 = f32[2,256,704]{1,2,0:T(8,128)} fusion(bf16[2,256,1024]{2,1,0:T(8,128)(2,1)} %bitcast.12, bf16[2,1024,704]{1,2,0:T(8,128)(2,1)} %param.23), kind=kOutput, calls=%fused_computation.72 | convolution fusion | flops 738197504 | bytes 5373952 | tf_op jit(solution)/shard_map/erd,edf->erf/dot_general | solution.py:43
  111.6 3.3 %fusion.57 = f32[2,256,704]{1,2,0:T(8,128)} fusion(bf16[2,256,1024]{2,1,0:T(8,128)(2,1)} %bitcast.17, bf16[2,1024,704]{1,2,0:T(8,128)(2,1)S(1)} %copy-done.1), kind=kOutput, calls=%fused_computation.73 | convolution fusion | flops 738197504 | bytes 5373952 | tf_op jit(solution)/shard_map/erd,edf->erf/dot_general | solution.py:44
  114.9 7.3 %fusion.6 = f32[2,256,1024]{2,1,0:T(8,128)} fusion(bf16[2,1024,704]{1,2,0:T(8,128)(2,1)} %param.23, bf16[2,256,1024]{2,1,0:T(8,128)(2,1)} %bitcast.22, bf16[2,1024,704]{1,2,0:T(8,128)(2,1)} %param.24, f32[2,256,704]{1,2,0:T(8,128)} %fusion.56, f32[2,256,704]{1,2,0:T(8,128)} %fusion.57), kind=kOutput, calls=%fused_computation.23 | convolution fusion | flops 1480720384 | bytes 11796480 | tf_op jit(solution)/shard_map/erf,edf->erd/dot_general | solution.py:49
  122.2 4.3 %fusion.58 = f32[2,256,704]{1,2,0:T(8,128)} fusion(bf16[2,256,1024]{2,1,0:T(8,128)(2,1)} %bitcast.12, bf16[2,1024,704]{1,2,0:T(8,128)(2,1)} %collective-permute-done), kind=kOutput, calls=%fused_computation.74 | convolution fusion | flops 738197504 | bytes 5373952 | tf_op jit(solution)/shard_map/erd,edf->erf/dot_general | solution.py:43
  126.6 3.4 %collective-permute-done.2 = bf16[2,256,1024]{2,1,0:T(8,128)(2,1)} collective-permute-done((bf16[2,256,1024]{2,1,0:T(8,128)(2,1)}, bf16[2,256,1024]{2,1,0:T(8,128)(2,1)}, u32[]{:S(2)}, u32[]{:S(2)}) %collective-permute-start.2) | collective-permute-done | bytes 1048608 | tf_op jit(solution)/shard_map/ppermute | solution.py:111
  130.0 3.3 %fusion.60 = f32[2,256,704]{1,2,0:T(8,128)} fusion(bf16[2,256,1024]{2,1,0:T(8,128)(2,1)} %collective-permute-done.2, bf16[2,1024,704]{1,2,0:T(8,128)(2,1)S(1)} %copy-done.2), kind=kOutput, calls=%fused_computation.76 | convolution fusion | flops 738197504 | bytes 5373952 | tf_op jit(solution)/shard_map/erd,edf->erf/dot_general | solution.py:43
  133.2 4.2 %fusion.62 = f32[2,256,704]{1,2,0:T(8,128)} fusion(bf16[2,256,1024]{2,1,0:T(8,128)(2,1)} %collective-permute-done.2, bf16[2,1024,704]{1,2,0:T(8,128)(2,1)} %collective-permute-done), kind=kOutput, calls=%fused_computation.78 | convolution fusion | flops 738197504 | bytes 5373952 | tf_op jit(solution)/shard_map/erd,edf->erf/dot_general | solution.py:43
  137.5 14.1 %collective-permute-done.3 = bf16[2,256,1024]{2,1,0:T(8,128)(2,1)} collective-permute-done((bf16[2,256,1024]{2,1,0:T(8,128)(2,1)}, bf16[2,256,1024]{2,1,0:T(8,128)(2,1)}, u32[]{:S(2)}, u32[]{:S(2)}) %collective-permute-start.3) | collective-permute-done | bytes 1048608 | tf_op jit(solution)/shard_map/ppermute | solution.py:111
  151.5 3.3 %fusion.61 = f32[2,256,704]{1,2,0:T(8,128)} fusion(bf16[2,256,1024]{2,1,0:T(8,128)(2,1)} %collective-permute-done.3, bf16[2,1024,704]{1,2,0:T(8,128)(2,1)S(1)} %copy-done.2), kind=kOutput, calls=%fused_computation.77 | convolution fusion | flops 738197504 | bytes 5373952 | tf_op jit(solution)/shard_map/erd,edf->erf/dot_general | solution.py:44
  154.8 4.2 %fusion.63 = f32[2,256,704]{1,2,0:T(8,128)} fusion(bf16[2,256,1024]{2,1,0:T(8,128)(2,1)} %collective-permute-done.3, bf16[2,1024,704]{1,2,0:T(8,128)(2,1)} %collective-permute-done), kind=kOutput, calls=%fused_computation.79 | convolution fusion | flops 738197504 | bytes 5373952 | tf_op jit(solution)/shard_map/erd,edf->erf/dot_general | solution.py:44
  159.0 7.4 %fusion.14 = f32[2,256,1024]{2,1,0:T(8,128)} fusion(bf16[2,1024,704]{1,2,0:T(8,128)(2,1)} %param.23, f32[2,256,704]{1,2,0:T(8,128)} %fusion.60, f32[2,256,704]{1,2,0:T(8,128)} %fusion.61, bf16[2,256,1024]{2,1,0:T(8,128)(2,1)} %collective-permute-done.4, bf16[2,1024,704]{1,2,0:T(8,128)(2,1)} %param.24), kind=kOutput, calls=%fused_computation.32 | convolution fusion | flops 1480720384 | bytes 11796480 | tf_op jit(solution)/shard_map/erf,edf->erd/dot_general | solution.py:49
  166.4 7.8 %add_convert_fusion.1 = bf16[2,256,1024]{2,1,0:T(8,128)(2,1)} fusion(f32[2,256,1024]{2,1,0:T(8,128)} %fusion.14, bf16[2,1024,704]{1,2,0:T(8,128)(2,1)} %collective-permute-done, f32[2,256,704]{1,2,0:T(8,128)} %fusion.62, f32[2,256,704]{1,2,0:T(8,128)} %fusion.63, bf16[2,256,1024]{2,1,0:T(8,128)(2,1)} %collective-permute-done.4, ...), kind=kOutput, calls=%fused_computation.2 | convolution fusion | flops 1481768960 | bytes 12845056 | tf_op jit(solution)/shard_map/erf,edf->erd/dot_general | solution.py:49
  174.2 1.5 collective-permute-start.5
  175.7 4.2 %fusion.59 = f32[2,256,704]{1,2,0:T(8,128)} fusion(bf16[2,256,1024]{2,1,0:T(8,128)(2,1)} %bitcast.17, bf16[2,1024,704]{1,2,0:T(8,128)(2,1)} %collective-permute-done), kind=kOutput, calls=%fused_computation.75 | convolution fusion | flops 738197504 | bytes 5373952 | tf_op jit(solution)/shard_map/erd,edf->erf/dot_general | solution.py:44
  179.9 7.4 %fusion.13 = f32[2,256,1024]{2,1,0:T(8,128)} fusion(bf16[2,1024,704]{1,2,0:T(8,128)(2,1)} %collective-permute-done, f32[2,256,704]{1,2,0:T(8,128)} %fusion.58, f32[2,256,704]{1,2,0:T(8,128)} %fusion.59, bf16[2,256,1024]{2,1,0:T(8,128)(2,1)} %bitcast.22, bf16[2,1024,704]{1,2,0:T(8,128)(2,1)} %collective-permute-done.1), kind=kOutput, calls=%fused_computation.31 | convolution fusion | flops 1480720384 | bytes 11796480 | tf_op jit(solution)/shard_map/erf,edf->erd/dot_general | solution.py:49
  187.3 11.5 %collective-permute-done.5 = bf16[2,256,1024]{2,1,0:T(8,128)(2,1)} collective-permute-done((bf16[2,256,1024]{2,1,0:T(8,128)(2,1)}, bf16[2,256,1024]{2,1,0:T(8,128)(2,1)}, u32[]{:S(2)}, u32[]{:S(2)}) %collective-permute-start.5) | collective-permute-done | bytes 1048608 | tf_op jit(solution)/shard_map/ppermute | solution.py:116
  198.8 3.1 %add_convert_fusion = bf16[2,256,1024]{2,1,0:T(8,128)(2,1)S(1)} fusion(bf16[2,256,1024]{2,1,0:T(8,128)(2,1)} %collective-permute-done.5, f32[2,256,1024]{2,1,0:T(8,128)} %fusion.6, f32[2,256,1024]{2,1,0:T(8,128)} %fusion.13), kind=kLoop, calls=%fused_computation.1 | loop fusion | flops 2097152 | bytes 6291456 | tf_op jit(solution)/shard_map/convert_element_type | solution.py:118
  202.0 1.1 copy.45
  203.0 29.5 %all_to_all.69 = bf16[2,256,1024]{2,0,1:T(2,128)(2,1)S(1)} all-to-all(bf16[2,256,1024]{2,0,1:T(2,128)(2,1)S(1)} %copy.45), channel_id=1, replica_groups=mesh['expert'=8,'dp'=4] {'expert'}, dimensions={1} | all-to-all | bytes 2097152 | tf_op jit(solution)/shard_map/all_to_all | solution.py:117
  232.5 0.3 copy.46
  232.8 0.1 copy.47
  232.9 1.3 fusion.5
  (18 shorter events, 0.1 us)
Async XLA Ops:
  0.0 8.5 %copy-start = (bf16[1024,1024]{1,0:T(8,128)(2,1)S(1)}, bf16[1024,1024]{1,0:T(8,128)(2,1)}, u32[]{:S(2)}) copy-start(bf16[1024,1024]{1,0:T(8,128)(2,1)} %param.25) | copy-start | bytes 6291460
  8.5 0.8 copy-start.5
  8.5 0.8 copy-start.6
  8.5 0.8 copy-start.4
  9.4 10.0 %copy-start.3 = (f32[1024]{0:T(1024)S(1)}, f32[1024]{0:T(1024)}, u32[]{:S(2)}) copy-start(f32[1024]{0:T(1024)} %param.22) | copy-start | bytes 12292
  10.9 33.2 %all-to-all-start.2 = ((bf16[16,32,1024]{2,1,0:T(8,128)(2,1)}), bf16[16,32,1024]{2,1,0:T(8,128)(2,1)}, u32[]{:S(2)}, u32[]{:S(2)}) async-start(bf16[16,32,1024]{2,1,0:T(8,128)(2,1)} %bitcast.78), calls=%async_computation.2 | async-start | bytes 2097152 | tf_op jit(solution)/shard_map/all_to_all | solution.py:90
  44.0 29.8 %all-to-all-start = ((bf16[16,32,1024]{2,1,0:T(8,128)(2,1)}), bf16[16,32,1024]{2,1,0:T(8,128)(2,1)}, u32[]{:S(2)}, u32[]{:S(2)}) async-start(bf16[16,32,1024]{2,1,0:T(8,128)(2,1)} %bitcast.82), calls=%async_computation | async-start | bytes 2097152 | tf_op jit(solution)/shard_map/all_to_all | solution.py:90
  73.8 29.7 %all-to-all-start.1 = ((bf16[16,32,1024]{2,1,0:T(8,128)(2,1)}), bf16[16,32,1024]{2,1,0:T(8,128)(2,1)}, u32[]{:S(2)}, u32[]{:S(2)}) async-start(bf16[16,32,1024]{2,1,0:T(8,128)(2,1)} %bitcast.81), calls=%async_computation.1 | async-start | bytes 2097152 | tf_op jit(solution)/shard_map/all_to_all | solution.py:90
  78.3 44.0 %collective-permute-start = (bf16[2,1024,704]{1,2,0:T(8,128)(2,1)}, bf16[2,1024,704]{1,2,0:T(8,128)(2,1)}, u32[]{:S(2)}, u32[]{:S(2)}) collective-permute-start(bf16[2,1024,704]{1,2,0:T(8,128)(2,1)} %param.23), channel_id=1, source_target_pairs={{0,1},{1,0},{2,3},{3,2},{4,5},{5,4},{6,7},{7,6},{8,9},{9,8},{10,11... | collective-permute-start | bytes 8650760 | tf_op jit(solution)/shard_map/ppermute | solution.py:77
  78.4 88.1 %collective-permute-start.1 = (bf16[2,1024,704]{1,2,0:T(8,128)(2,1)}, bf16[2,1024,704]{1,2,0:T(8,128)(2,1)}, u32[]{:S(2)}, u32[]{:S(2)}) collective-permute-start(bf16[2,1024,704]{1,2,0:T(8,128)(2,1)} %param.24), channel_id=1, source_target_pairs={{0,1},{1,0},{2,3},{3,2},{4,5},{5,4},{6,7},{7,6},{8,9},{9,8},{10,11... | collective-permute-start | bytes 8650760 | tf_op jit(solution)/shard_map/ppermute | solution.py:77
  81.1 77.9 %collective-permute-start.4 = (bf16[2,256,1024]{2,1,0:T(8,128)(2,1)}, bf16[2,256,1024]{2,1,0:T(8,128)(2,1)}, u32[]{:S(2)}, u32[]{:S(2)}) collective-permute-start(bf16[2,256,1024]{2,1,0:T(8,128)(2,1)} %bitcast.22), channel_id=1, source_target_pairs={{0,2},{1,3},{2,0},{3,1},{4,6},{5,7},{6,4},{7,5},{8,10},{9,11},{10,... | collective-permute-start | bytes 3145736 | tf_op jit(solution)/shard_map/ppermute | solution.py:111
  85.0 45.0 %collective-permute-start.2 = (bf16[2,256,1024]{2,1,0:T(8,128)(2,1)}, bf16[2,256,1024]{2,1,0:T(8,128)(2,1)}, u32[]{:S(2)}, u32[]{:S(2)}) collective-permute-start(bf16[2,256,1024]{2,1,0:T(8,128)(2,1)} %bitcast.12), channel_id=1, source_target_pairs={{0,2},{1,3},{2,0},{3,1},{4,6},{5,7},{6,4},{7,5},{8,10},{9,11},{10,... | collective-permute-start | bytes 3145736 | tf_op jit(solution)/shard_map/ppermute | solution.py:111
  105.8 5.8 %copy-start.1 = (bf16[2,1024,704]{1,2,0:T(8,128)(2,1)S(1)}, bf16[2,1024,704]{1,2,0:T(8,128)(2,1)}, u32[]{:S(2)}) copy-start(bf16[2,1024,704]{1,2,0:T(8,128)(2,1)} %param.23) | copy-start | bytes 8650756
  105.8 45.7 %collective-permute-start.3 = (bf16[2,256,1024]{2,1,0:T(8,128)(2,1)}, bf16[2,256,1024]{2,1,0:T(8,128)(2,1)}, u32[]{:S(2)}, u32[]{:S(2)}) collective-permute-start(bf16[2,256,1024]{2,1,0:T(8,128)(2,1)} %bitcast.17), channel_id=1, source_target_pairs={{0,2},{1,3},{2,0},{3,1},{4,6},{5,7},{6,4},{7,5},{8,10},{9,11},{10,... | collective-permute-start | bytes 3145736 | tf_op jit(solution)/shard_map/ppermute | solution.py:111
  122.2 7.7 %copy-start.2 = (bf16[2,1024,704]{1,2,0:T(8,128)(2,1)S(1)}, bf16[2,1024,704]{1,2,0:T(8,128)(2,1)}, u32[]{:S(2)}) copy-start(bf16[2,1024,704]{1,2,0:T(8,128)(2,1)} %param.23) | copy-start | bytes 8650756
  174.2 24.6 %collective-permute-start.5 = (bf16[2,256,1024]{2,1,0:T(8,128)(2,1)}, bf16[2,256,1024]{2,1,0:T(8,128)(2,1)}, u32[]{:S(2)}, u32[]{:S(2)}) collective-permute-start(bf16[2,256,1024]{2,1,0:T(8,128)(2,1)} %add_convert_fusion.1), channel_id=1, source_target_pairs={{2,0},{3,1},{0,2},{1,3},{6,4},{7,5},{4,6},{5,7},{10,8},{11,9},{8,1... | collective-permute-start | bytes 3145736 | tf_op jit(solution)/shard_map/ppermute | solution.py:116
where the time goes:
time: 235 us; the launch traced here: 234 us
  waiting for transfers between devices  92.1 us (39%)
  matrix products  73.8 us (31%)
  blocking collectives  29.5 us (13%)
  starting transfers between devices  21.6 us (9%)
  local copies, waits for them, and re-layouts  12 us (5%)
  other arithmetic  4.38 us (2%)
    all_to_all x3, waiting for transfers between devices, dispatch(): lax.all_to_all(placed, 'expert', split_axis=0, concat_axis=1, tiled=True)  63.1 us
    dot_general x4, matrix products, expert_terms(): jnp.einsum('erf,edf->erd', act_mult, part_in, preferred_element_type=jnp....  29.8 us
    all_to_all x1, blocking collectives, body(): lax.all_to_all(slot_mult.astype(jnp.bfloat16), 'expert', split_axis=1, co...  29.5 us
    ppermute x3, waiting for transfers between devices, body(): far_rows.append(tuple((lax.ppermute(a, 'dp', ahead) for a in own_rows)))  17.5 us
    dot_general x4, matrix products, expert_terms(): jnp.einsum('erd,edf->erf', rows_in, part_in, preferred_element_type=jnp.f...  16.1 us
    all_to_all x3, starting transfers between devices, dispatch(): lax.all_to_all(placed, 'expert', split_axis=0, concat_axis=1, tiled=True)  15.9 us
    dot_general x4, matrix products, expert_terms(): jnp.einsum('erd,edf->erf', rows_base, part_in, preferred_element_type=jnp...  15 us
    ppermute x1, waiting for transfers between devices, body(): lax.ppermute(far_part, 'dp', back).astype(jnp.float32)  11.5 us
  transfers between devices with their start and end apart: 9, of which 6 were waited for; matrix products, arithmetic and copies ran while one was open for 28% of the time, Pallas kernels for 0%

commit v1 on v0

--- a/solution.py
+++ b/solution.py
@@ -87,7 +87,12 @@
     def dispatch(values):
         placed = jnp.dot(onehot, values, preferred_element_type=jnp.float32).astype(jnp.bfloat16)
         placed = placed.reshape(n_experts, capacity, feature_width)
-        return lax.all_to_all(placed, "expert", split_axis=0, concat_axis=1, tiled=True)
+        return jnp.concatenate(
+            lax.all_to_all(
+                jnp.stack(jnp.split(placed, lax.axis_size("expert"), axis=0)), "expert", 0, 0
+            ),
+            axis=1,
+        )
 
     sent_in = dispatch(inputs)
     sent_base = dispatch(base_inputs)

time: 235 us -> 226 us (0.962)
  waiting for transfers between devices: 92.1 us -> 66.5 us
  local copies, waits for them, and re-layouts: 12 us -> 29.1 us
    all_to_all x3, waiting for transfers between devices: 63.1 us -> 45 us  [dispatch(): lax.all_to_all(jnp.stack(jnp.split(placed, lax.axis_size('expert'), axis=...]
    unnamed x17 -> x40, local copies, waits for them, and re-layouts: 3.67 us -> 18.5 us
    ppermute x3, waiting for transfers between devices: 17.5 us -> 9.98 us  [body(): far_rows.append(tuple((lax.ppermute(a, 'dp', ahead) for a in own_rows)))]
    reshape x0 -> x2, local copies, waits for them, and re-layouts: none -> 4.61 us  [dispatch(): jnp.concatenate(lax.all_to_all(jnp.stack(jnp.split(placed, lax.axis_size(...]
    all_to_all x3 -> x1, local copies, waits for them, and re-layouts: 6.87 us -> 2.29 us  [dispatch(): lax.all_to_all(jnp.stack(jnp.split(placed, lax.axis_size('expert'), axis=...]
    dot_general x3, matrix products: 6.64 us -> 3.72 us  [dispatch(): jnp.dot(onehot, values, preferred_element_type=jnp.float32)]
  transfers between devices with their start and end apart: 9 -> 9, of which waited for: 6 -> 5; matrix products, arithmetic and copies ran while one was open for 28% -> 37% of each run, Pallas kernels for 0% -> 0%
where the time goes in v1:
time: 226 us; the launch traced here: 225 us
  matrix products  72.1 us (32%)
  waiting for transfers between devices  66.5 us (29%)
  blocking collectives  29.5 us (13%)
  local copies, waits for them, and re-layouts  29.1 us (13%)
  starting transfers between devices  21.7 us (10%)
  other arithmetic  5.23 us (2%)
    all_to_all x3, waiting for transfers between devices, dispatch(): lax.all_to_all(jnp.stack(jnp.split(placed, lax.axis_size('expert'), axis=...  45 us
    dot_general x4, matrix products, expert_terms(): jnp.einsum('erf,edf->erd', act_mult, part_in, preferred_element_type=jnp....  29.8 us
    all_to_all x1, blocking collectives, body(): lax.all_to_all(slot_mult.astype(jnp.bfloat16), 'expert', split_axis=1, co...  29.5 us
    unnamed x40, local copies, waits for them, and re-layouts  18.5 us
    dot_general x4, matrix products, expert_terms(): jnp.einsum('erd,edf->erf', rows_in, part_in, preferred_element_type=jnp.f...  16.1 us
    all_to_all x3, starting transfers between devices, dispatch(): lax.all_to_all(jnp.stack(jnp.split(placed, lax.axis_size('expert'), axis=...  16.1 us
    dot_general x4, matrix products, expert_terms(): jnp.einsum('erd,edf->erf', rows_base, part_in, preferred_element_type=jnp...  15 us
    ppermute x1, waiting for transfers between devices, body(): lax.ppermute(far_part, 'dp', back).astype(jnp.float32)  11.5 us
  transfers between devices with their start and end apart: 9, of which 5 were waited for; matrix products, arithmetic and copies ran while one was open for 37% of the time, Pallas kernels for 0%

profile of v1, /device:TPU:0, one launch (start us, length us, event | category | flops | bytes accessed | tf_op | source)
XLA Modules:
  0.0 225.0 jit_solution(15283952869562136812)
XLA Ops:
  0.0 1.4 fusion.7
  1.4 0.7 multiply_add_fusion
  2.1 1.6 convolution_convert_fusion.2
  4.5 0.7 constant_dynamic-update-slice_fusion.6
  5.8 0.7 constant_dynamic-update-slice_fusion.4
  7.1 0.7 constant_dynamic-update-slice_fusion.2
  9.1 7.4 %all-to-all-start = ((bf16[8,2,32,1024]{3,2,1,0:T(8,128)(2,1)}), bf16[8,2,32,1024]{3,2,1,0:T(8,128)(2,1)S(1)}, u32[]{:S(2)}, u32[]{:S(2)}) async-start(bf16[8,2,32,1024]{3,2,1,0:T(8,128)(2,1)} %constant_dynamic-update-slice_fusion), calls=%async_computation | async-start | bytes 2097152 | tf_op jit(solution)/shard_map/all_to_all | solution.py:91
  16.5 0.8 copy.42
  18.0 1.8 copy.40
  19.8 2.0 copy.41
  21.8 1.6 convolution_convert_fusion.1
  23.6 0.7 constant_dynamic-update-slice_fusion.15
  26.8 0.7 constant_dynamic-update-slice_fusion.10
  28.8 3.2 %fusion.51 = (f32[16,128]{1,0:T(8,128)S(1)}, f32[16,128,256]{2,1,0:T(8,128)}) fusion(pred[256]{0:T(512)(128)(4,1)S(1)} %iota_compare_fusion.5, bf16[128,16,64]{0,2,1:T(8,128)(2,1)} %bitcast.124, bf16[256,16,64]{0,2,1:T(8,128)(2,1)} %bitcast.122), kind=kOutput, calls=%fused_computation.94 | convolution fusion | flops 69206272 | bytes 2892032 | tf_op jit(solution)/shard_map/sub | solution.py:29
  32.0 10.3 %all-to-all-done = bf16[8,2,32,1024]{3,2,1,0:T(8,128)(2,1)S(1)} async-done(((bf16[8,2,32,1024]{3,2,1,0:T(8,128)(2,1)}), bf16[8,2,32,1024]{3,2,1,0:T(8,128)(2,1)S(1)}, u32[]{:S(2)}, u32[]{:S(2)}) %all-to-all-start) | async-done | bytes 1048608 | tf_op jit(solution)/shard_map/all_to_all | solution.py:91
  42.3 4.2 %all-to-all-start.1 = ((bf16[8,2,32,1024]{3,2,1,0:T(8,128)(2,1)}), bf16[8,2,32,1024]{3,2,1,0:T(8,128)(2,1)}, u32[]{:S(2)}, u32[]{:S(2)}) async-start(bf16[8,2,32,1024]{3,2,1,0:T(8,128)(2,1)} %constant_dynamic-update-slice_fusion.8), calls=%async_computation.1 | async-start | bytes 2097152 | tf_op jit(solution)/shard_map/all_to_all | solution.py:91
  46.5 2.1 convolution_convert_fusion.3
  48.7 0.8 fusion.58
  50.1 0.7 constant_dynamic-update-slice_fusion.23
  51.4 0.7 constant_dynamic-update-slice_fusion.21
  54.1 0.7 constant_dynamic-update-slice_fusion.17
  55.4 16.7 %all-to-all-done.1 = bf16[8,2,32,1024]{3,2,1,0:T(8,128)(2,1)} async-done(((bf16[8,2,32,1024]{3,2,1,0:T(8,128)(2,1)}), bf16[8,2,32,1024]{3,2,1,0:T(8,128)(2,1)}, u32[]{:S(2)}, u32[]{:S(2)}) %all-to-all-start.1) | async-done | bytes 1048608 | tf_op jit(solution)/shard_map/all_to_all | solution.py:91
  72.1 4.4 %all-to-all-start.2 = ((bf16[8,2,32,1024]{3,2,1,0:T(8,128)(2,1)}), bf16[8,2,32,1024]{3,2,1,0:T(8,128)(2,1)}, u32[]{:S(2)}, u32[]{:S(2)}) async-start(bf16[8,2,32,1024]{3,2,1,0:T(8,128)(2,1)} %constant_dynamic-update-slice_fusion.16), calls=%async_computation.2 | async-start | bytes 2097152 | tf_op jit(solution)/shard_map/all_to_all | solution.py:91
  77.1 2.3 %copy.43 = bf16[2,8,32,1024]{3,2,1,0:T(8,128)(2,1)} copy(bf16[2,8,32,1024]{3,2,0,1:T(8,128)(2,1)} %bitcast.94) | data formatting | bytes 2097152 | tf_op jit(solution)/shard_map/reshape | solution.py:90
  79.4 1.5 collective-permute-start.2
  80.9 2.3 %copy.44 = bf16[2,8,32,1024]{3,2,1,0:T(8,128)(2,1)} copy(bf16[2,8,32,1024]{3,2,0,1:T(8,128)(2,1)} %bitcast.28) | data formatting | bytes 2097152 | tf_op jit(solution)/shard_map/reshape | solution.py:90
  83.7 18.0 %all-to-all-done.2 = bf16[8,2,32,1024]{3,2,1,0:T(8,128)(2,1)} async-done(((bf16[8,2,32,1024]{3,2,1,0:T(8,128)(2,1)}), bf16[8,2,32,1024]{3,2,1,0:T(8,128)(2,1)}, u32[]{:S(2)}, u32[]{:S(2)}) %all-to-all-start.2) | async-done | bytes 1048608 | tf_op jit(solution)/shard_map/all_to_all | solution.py:91
  101.8 2.3 %copy.45 = bf16[8,2,32,1024]{3,2,0,1:T(8,128)(2,1)} copy(bf16[8,2,32,1024]{3,2,1,0:T(8,128)(2,1)} %all-to-all-done.2) | data formatting | bytes 2097152 | tf_op jit(solution)/shard_map/all_to_all | solution.py:91
  104.1 1.5 collective-permute-start.4
  105.6 4.3 %fusion.59 = f32[2,256,704]{1,2,0:T(8,128)} fusion(bf16[2,256,1024]{2,1,0:T(8,128)(2,1)} %bitcast.18, bf16[2,1024,704]{1,2,0:T(8,128)(2,1)} %param.23), kind=kOutput, calls=%fused_computation.99 | convolution fusion | flops 738197504 | bytes 5373952 | tf_op jit(solution)/shard_map/erd,edf->erf/dot_general | solution.py:43
  109.9 3.3 %fusion.60 = f32[2,256,704]{1,2,0:T(8,128)} fusion(bf16[2,256,1024]{2,1,0:T(8,128)(2,1)} %bitcast.29, bf16[2,1024,704]{1,2,0:T(8,128)(2,1)S(1)} %copy-done.1), kind=kOutput, calls=%fused_computation.100 | convolution fusion | flops 738197504 | bytes 5373952 | tf_op jit(solution)/shard_map/erd,edf->erf/dot_general | solution.py:44
  113.2 7.3 %fusion.6 = f32[2,256,1024]{2,1,0:T(8,128)} fusion(bf16[2,1024,704]{1,2,0:T(8,128)(2,1)} %param.23, bf16[2,256,1024]{2,1,0:T(8,128)(2,1)} %bitcast.40, bf16[2,1024,704]{1,2,0:T(8,128)(2,1)} %param.24, f32[2,256,704]{1,2,0:T(8,128)} %fusion.59, f32[2,256,704]{1,2,0:T(8,128)} %fusion.60), kind=kOutput, calls=%fused_computation.23 | convolution fusion | flops 1480720384 | bytes 11796480 | tf_op jit(solution)/shard_map/erf,edf->erd/dot_general | solution.py:49
  120.5 4.3 %fusion.61 = f32[2,256,704]{1,2,0:T(8,128)} fusion(bf16[2,256,1024]{2,1,0:T(8,128)(2,1)} %bitcast.18, bf16[2,1024,704]{1,2,0:T(8,128)(2,1)} %collective-permute-done), kind=kOutput, calls=%fused_computation.101 | convolution fusion | flops 738197504 | bytes 5373952 | tf_op jit(solution)/shard_map/erd,edf->erf/dot_general | solution.py:43
  124.8 3.3 %fusion.63 = f32[2,256,704]{1,2,0:T(8,128)} fusion(bf16[2,256,1024]{2,1,0:T(8,128)(2,1)} %collective-permute-done.2, bf16[2,1024,704]{1,2,0:T(8,128)(2,1)S(1)} %copy-done.2), kind=kOutput, calls=%fused_computation.103 | convolution fusion | flops 738197504 | bytes 5373952 | tf_op jit(solution)/shard_map/erd,edf->erf/dot_general | solution.py:43
  128.1 4.2 %fusion.65 = f32[2,256,704]{1,2,0:T(8,128)} fusion(bf16[2,256,1024]{2,1,0:T(8,128)(2,1)} %collective-permute-done.2, bf16[2,1024,704]{1,2,0:T(8,128)(2,1)} %collective-permute-done), kind=kOutput, calls=%fused_computation.105 | convolution fusion | flops 738197504 | bytes 5373952 | tf_op jit(solution)/shard_map/erd,edf->erf/dot_general | solution.py:43
  132.4 3.3 %fusion.64 = f32[2,256,704]{1,2,0:T(8,128)} fusion(bf16[2,256,1024]{2,1,0:T(8,128)(2,1)} %collective-permute-done.3, bf16[2,1024,704]{1,2,0:T(8,128)(2,1)S(1)} %copy-done.2), kind=kOutput, calls=%fused_computation.104 | convolution fusion | flops 738197504 | bytes 5373952 | tf_op jit(solution)/shard_map/erd,edf->erf/dot_general | solution.py:44
  135.6 4.2 %fusion.66 = f32[2,256,704]{1,2,0:T(8,128)} fusion(bf16[2,256,1024]{2,1,0:T(8,128)(2,1)} %collective-permute-done.3, bf16[2,1024,704]{1,2,0:T(8,128)(2,1)} %collective-permute-done), kind=kOutput, calls=%fused_computation.106 | convolution fusion | flops 738197504 | bytes 5373952 | tf_op jit(solution)/shard_map/erd,edf->erf/dot_general | solution.py:44
  139.8 10.0 %collective-permute-done.4 = bf16[2,256,1024]{2,1,0:T(8,128)(2,1)} collective-permute-done((bf16[2,256,1024]{2,1,0:T(8,128)(2,1)}, bf16[2,256,1024]{2,1,0:T(8,128)(2,1)}, u32[]{:S(2)}, u32[]{:S(2)}) %collective-permute-start.4) | collective-permute-done | bytes 1048608 | tf_op jit(solution)/shard_map/ppermute | solution.py:116
  149.8 7.4 %fusion.14 = f32[2,256,1024]{2,1,0:T(8,128)} fusion(bf16[2,1024,704]{1,2,0:T(8,128)(2,1)} %param.23, f32[2,256,704]{1,2,0:T(8,128)} %fusion.63, f32[2,256,704]{1,2,0:T(8,128)} %fusion.64, bf16[2,256,1024]{2,1,0:T(8,128)(2,1)} %collective-permute-done.4, bf16[2,1024,704]{1,2,0:T(8,128)(2,1)} %param.24), kind=kOutput, calls=%fused_computation.32 | convolution fusion | flops 1480720384 | bytes 11796480 | tf_op jit(solution)/shard_map/erf,edf->erd/dot_general | solution.py:49
  157.2 7.8 %add_convert_fusion.1 = bf16[2,256,1024]{2,1,0:T(8,128)(2,1)} fusion(f32[2,256,1024]{2,1,0:T(8,128)} %fusion.14, bf16[2,1024,704]{1,2,0:T(8,128)(2,1)} %collective-permute-done, f32[2,256,704]{1,2,0:T(8,128)} %fusion.65, f32[2,256,704]{1,2,0:T(8,128)} %fusion.66, bf16[2,256,1024]{2,1,0:T(8,128)(2,1)} %collective-permute-done.4, ...), kind=kOutput, calls=%fused_computation.2 | convolution fusion | flops 1481768960 | bytes 12845056 | tf_op jit(solution)/shard_map/erf,edf->erd/dot_general | solution.py:49
  165.0 1.5 collective-permute-start.5
  166.5 4.2 %fusion.62 = f32[2,256,704]{1,2,0:T(8,128)} fusion(bf16[2,256,1024]{2,1,0:T(8,128)(2,1)} %bitcast.29, bf16[2,1024,704]{1,2,0:T(8,128)(2,1)} %collective-permute-done), kind=kOutput, calls=%fused_computation.102 | convolution fusion | flops 738197504 | bytes 5373952 | tf_op jit(solution)/shard_map/erd,edf->erf/dot_general | solution.py:44
  170.7 7.4 %fusion.13 = f32[2,256,1024]{2,1,0:T(8,128)} fusion(bf16[2,1024,704]{1,2,0:T(8,128)(2,1)} %collective-permute-done, f32[2,256,704]{1,2,0:T(8,128)} %fusion.61, f32[2,256,704]{1,2,0:T(8,128)} %fusion.62, bf16[2,256,1024]{2,1,0:T(8,128)(2,1)} %bitcast.40, bf16[2,1024,704]{1,2,0:T(8,128)(2,1)} %collective-permute-done.1), kind=kOutput, calls=%fused_computation.31 | convolution fusion | flops 1480720384 | bytes 11796480 | tf_op jit(solution)/shard_map/erf,edf->erd/dot_general | solution.py:49
  178.1 11.5 %collective-permute-done.5 = bf16[2,256,1024]{2,1,0:T(8,128)(2,1)} collective-permute-done((bf16[2,256,1024]{2,1,0:T(8,128)(2,1)}, bf16[2,256,1024]{2,1,0:T(8,128)(2,1)}, u32[]{:S(2)}, u32[]{:S(2)}) %collective-permute-start.5) | collective-permute-done | bytes 1048608 | tf_op jit(solution)/shard_map/ppermute | solution.py:121
  189.6 3.1 %add_convert_fusion = bf16[2,256,1024]{2,1,0:T(8,128)(2,1)S(1)} fusion(bf16[2,256,1024]{2,1,0:T(8,128)(2,1)} %collective-permute-done.5, f32[2,256,1024]{2,1,0:T(8,128)} %fusion.6, f32[2,256,1024]{2,1,0:T(8,128)} %fusion.13), kind=kLoop, calls=%fused_computation.1 | loop fusion | flops 2097152 | bytes 6291456 | tf_op jit(solution)/shard_map/convert_element_type | solution.py:123
  192.7 1.1 copy.46
  193.8 29.5 %all_to_all.30 = bf16[2,256,1024]{2,0,1:T(2,128)(2,1)S(1)} all-to-all(bf16[2,256,1024]{2,0,1:T(2,128)(2,1)S(1)} %copy.46), channel_id=1, replica_groups=mesh['expert'=8,'dp'=4] {'expert'}, dimensions={1} | all-to-all | bytes 2097152 | tf_op jit(solution)/shard_map/all_to_all | solution.py:122
  223.7 1.3 fusion.5
  (47 shorter events, 12.7 us)
Async XLA Ops:
  0.0 48.7 %copy-start = (bf16[1024,1024]{1,0:T(8,128)(2,1)S(1)}, bf16[1024,1024]{1,0:T(8,128)(2,1)}, u32[]{:S(2)}) copy-start(bf16[1024,1024]{1,0:T(8,128)(2,1)} %param.25) | copy-start | bytes 6291460
  3.8 12.7 %copy-start.4 = (bf16[1,1,128,1024]{3,2,1,0:T(8,128)(2,1)S(1)}, bf16[1,1,128,1024]{3,2,1,0:T(8,128)(2,1)}, u32[]{:S(2)}) copy-start(bf16[1,1,128,1024]{3,2,1,0:T(8,128)(2,1)} %param.17) | copy-start | bytes 786436
  9.1 12.8 %copy-start.6 = (f32[1024]{0:T(1024)S(1)}, f32[1024]{0:T(1024)}, u32[]{:S(2)}) copy-start(f32[1024]{0:T(1024)} %param.22) | copy-start | bytes 12292
  9.1 33.2 %all-to-all-start = ((bf16[8,2,32,1024]{3,2,1,0:T(8,128)(2,1)}), bf16[8,2,32,1024]{3,2,1,0:T(8,128)(2,1)S(1)}, u32[]{:S(2)}, u32[]{:S(2)}) async-start(bf16[8,2,32,1024]{3,2,1,0:T(8,128)(2,1)} %constant_dynamic-update-slice_fusion), calls=%async_computation | async-start | bytes 2097152 | tf_op jit(solution)/shard_map/all_to_all | solution.py:91
  28.8 17.7 %copy-start.5 = (bf16[1,1,128,1024]{2,3,1,0:T(8,128)(2,1)S(1)}, bf16[1,1,128,1024]{2,3,1,0:T(8,128)(2,1)}, u32[]{:S(2)}) copy-start(bf16[1,1,128,1024]{2,3,1,0:T(8,128)(2,1)} %copy.42) | copy-start | bytes 786436
  42.3 6.4 %copy-start.3 = (bf16[8,2,32,1024]{3,2,1,0:T(8,128)(2,1)}, bf16[8,2,32,1024]{3,2,1,0:T(8,128)(2,1)S(1)}, u32[]{:S(2)}) copy-start(bf16[8,2,32,1024]{3,2,1,0:T(8,128)(2,1)S(1)} %all-to-all-done) | copy-start | bytes 3145732
  42.3 29.8 %all-to-all-start.1 = ((bf16[8,2,32,1024]{3,2,1,0:T(8,128)(2,1)}), bf16[8,2,32,1024]{3,2,1,0:T(8,128)(2,1)}, u32[]{:S(2)}, u32[]{:S(2)}) async-start(bf16[8,2,32,1024]{3,2,1,0:T(8,128)(2,1)} %constant_dynamic-update-slice_fusion.8), calls=%async_computation.1 | async-start | bytes 2097152 | tf_op jit(solution)/shard_map/all_to_all | solution.py:91
  48.7 0.8 copy-start.7
  72.1 29.7 %all-to-all-start.2 = ((bf16[8,2,32,1024]{3,2,1,0:T(8,128)(2,1)}), bf16[8,2,32,1024]{3,2,1,0:T(8,128)(2,1)}, u32[]{:S(2)}, u32[]{:S(2)}) async-start(bf16[8,2,32,1024]{3,2,1,0:T(8,128)(2,1)} %constant_dynamic-update-slice_fusion.16), calls=%async_computation.2 | async-start | bytes 2097152 | tf_op jit(solution)/shard_map/all_to_all | solution.py:91
  76.5 44.0 %collective-permute-start = (bf16[2,1024,704]{1,2,0:T(8,128)(2,1)}, bf16[2,1024,704]{1,2,0:T(8,128)(2,1)}, u32[]{:S(2)}, u32[]{:S(2)}) collective-permute-start(bf16[2,1024,704]{1,2,0:T(8,128)(2,1)} %param.23), channel_id=1, source_target_pairs={{0,1},{1,0},{2,3},{3,2},{4,5},{5,4},{6,7},{7,6},{8,9},{9,8},{10,11... | collective-permute-start | bytes 8650760 | tf_op jit(solution)/shard_map/ppermute | solution.py:77
  76.6 80.6 %collective-permute-start.1 = (bf16[2,1024,704]{1,2,0:T(8,128)(2,1)}, bf16[2,1024,704]{1,2,0:T(8,128)(2,1)}, u32[]{:S(2)}, u32[]{:S(2)}) collective-permute-start(bf16[2,1024,704]{1,2,0:T(8,128)(2,1)} %param.24), channel_id=1, source_target_pairs={{0,1},{1,0},{2,3},{3,2},{4,5},{5,4},{6,7},{7,6},{8,9},{9,8},{10,11... | collective-permute-start | bytes 8650760 | tf_op jit(solution)/shard_map/ppermute | solution.py:77
  79.4 45.4 %collective-permute-start.2 = (bf16[2,256,1024]{2,1,0:T(8,128)(2,1)}, bf16[2,256,1024]{2,1,0:T(8,128)(2,1)}, u32[]{:S(2)}, u32[]{:S(2)}) collective-permute-start(bf16[2,256,1024]{2,1,0:T(8,128)(2,1)} %bitcast.18), channel_id=1, source_target_pairs={{0,2},{1,3},{2,0},{3,1},{4,6},{5,7},{6,4},{7,5},{8,10},{9,11},{10,... | collective-permute-start | bytes 3145736 | tf_op jit(solution)/shard_map/ppermute | solution.py:116
  83.2 49.1 %collective-permute-start.3 = (bf16[2,256,1024]{2,1,0:T(8,128)(2,1)}, bf16[2,256,1024]{2,1,0:T(8,128)(2,1)}, u32[]{:S(2)}, u32[]{:S(2)}) collective-permute-start(bf16[2,256,1024]{2,1,0:T(8,128)(2,1)} %bitcast.29), channel_id=1, source_target_pairs={{0,2},{1,3},{2,0},{3,1},{4,6},{5,7},{6,4},{7,5},{8,10},{9,11},{10,... | collective-permute-start | bytes 3145736 | tf_op jit(solution)/shard_map/ppermute | solution.py:116
  104.1 5.8 %copy-start.1 = (bf16[2,1024,704]{1,2,0:T(8,128)(2,1)S(1)}, bf16[2,1024,704]{1,2,0:T(8,128)(2,1)}, u32[]{:S(2)}) copy-start(bf16[2,1024,704]{1,2,0:T(8,128)(2,1)} %param.23) | copy-start | bytes 8650756
  104.1 45.7 %collective-permute-start.4 = (bf16[2,256,1024]{2,1,0:T(8,128)(2,1)}, bf16[2,256,1024]{2,1,0:T(8,128)(2,1)}, u32[]{:S(2)}, u32[]{:S(2)}) collective-permute-start(bf16[2,256,1024]{2,1,0:T(8,128)(2,1)} %bitcast.40), channel_id=1, source_target_pairs={{0,2},{1,3},{2,0},{3,1},{4,6},{5,7},{6,4},{7,5},{8,10},{9,11},{10,... | collective-permute-start | bytes 3145736 | tf_op jit(solution)/shard_map/ppermute | solution.py:116
  120.5 4.3 %copy-start.2 = (bf16[2,1024,704]{1,2,0:T(8,128)(2,1)S(1)}, bf16[2,1024,704]{1,2,0:T(8,128)(2,1)}, u32[]{:S(2)}) copy-start(bf16[2,1024,704]{1,2,0:T(8,128)(2,1)} %param.23) | copy-start | bytes 8650756
  165.0 24.6 %collective-permute-start.5 = (bf16[2,256,1024]{2,1,0:T(8,128)(2,1)}, bf16[2,256,1024]{2,1,0:T(8,128)(2,1)}, u32[]{:S(2)}, u32[]{:S(2)}) collective-permute-start(bf16[2,256,1024]{2,1,0:T(8,128)(2,1)} %add_convert_fusion.1), channel_id=1, source_target_pairs={{2,0},{3,1},{0,2},{1,3},{6,4},{7,5},{4,6},{5,7},{10,8},{11,9},{8,1... | collective-permute-start | bytes 3145736 | tf_op jit(solution)/shard_map/ppermute | solution.py:121
